TPU v7x, 128 devices: a whole 4x4x4 slice. The times are simulated.
128 devices in a mesh: grp: 4 (over y_hi, core), req: 32 (over x, z, y_lo).
Axes of the slice: x: 4, y: 4 (y_hi: 2, y_lo: 2; y = y_hi * 2 + y_lo), z: 4, core: 2. Of those that a mesh axis runs over, the one named last changes fastest.
Arguments:
- tokens: bfloat16 [16384, 1024], P(('grp', 'req')), may hold values from -6 to 6
- attn_gain: float32 [1024], replicated, may hold values from 0.1 to 1.9
- w_query: bfloat16 [1024, 1024], replicated, may hold values from -0.0234375 to 0.0234375
- w_key: bfloat16 [1024, 1024], replicated, may hold values from -0.1875 to 0.1875
- w_value: bfloat16 [1024, 1024], replicated, may hold values from -0.1875 to 0.1875
- w_attn_out: bfloat16 [1024, 1024], replicated, may hold values from -0.1875 to 0.1875
- rel_bias: float32 [32, 16], replicated, may hold values from -4 to 4
- prefix_cache: bfloat16 [8, 512, 2048], P('grp', 'req'), may hold values from -6 to 6
- lengths: int32 [4, 64], P('grp'), may hold values from 1 to 128, 4096 in all within a row
- prefix_map: int32 [4, 64], P('grp'), may hold values from 0 to 1
- mlp_gain: float32 [1024], replicated, may hold values from 0.1 to 1.9
- w_in: bfloat16 [4096, 1024], P('grp'), may hold values from -0.1875 to 0.1875
- w_out: bfloat16 [4096, 1024], P('grp'), may hold values from -0.09375 to 0.09375
Outputs:
- layer_out: bfloat16 [16384, 1024], P(('grp', 'req'))
Inputs may be any that keep to these rules, and one draw needn't show every extreme that they name: In each group the lengths sum to 4096 and the longest is exactly 128.
All inputs are finite; a program needn't handle non-finite values.
Results may differ from a plain program's by a relative error of at most 0.017.
Values may be sent and summed in bfloat16 or wider, within the bound.
No kernel may reach another device: no remote copies, remote signals or barrier semaphores. Data moves between devices by JAX's collectives and lax.ppermute only.
A program may use at most 128 MiB of HBM per device.

v0:
```python
import jax
import jax.numpy as jnp
from jax import lax
from jax.sharding import PartitionSpec as P

D = 1024
H = 16
DK = 64
PLEN = 512
PREF_GRP = 2
epsilon = 1e-06
far_marks = (12, 16, 23, 32, 46, 64, 91)
masked_score = -1e30


def padded(value, sides, width):
    for axis, dim in sides:
        count, length = (lax.axis_size(axis), value.shape[dim])
        up = [(i, (i + 1) % count) for i in range(count - 1)]
        down = [(j, i) for i, j in up]
        last = lax.slice_in_dim(value, length - width, length, axis=dim)
        leading = lax.slice_in_dim(value, 0, width, axis=dim)
        before = lax.ppermute(last, axis, up)
        after = lax.ppermute(leading, axis, down)
        value = jnp.concatenate([before, value, after], axis=dim)
    return value


def bucket_of(relative):
    distance = jnp.abs(relative)
    far_bucket = 8 + sum([(distance >= threshold).astype(jnp.int32) for threshold in far_marks])
    bucket = jnp.where(distance < 8, distance, far_bucket)
    return bucket + jnp.where(relative > 0, 16, 0)


def bias_lookup(relative, rel_bias):
    buckets = bucket_of(relative)
    marks = jnp.arange(rel_bias.shape[0], dtype=jnp.int32)
    one_hot = (buckets[:, :, None] == marks[None, None, :]).astype(jnp.float32)
    return jnp.einsum(
        "qkb,bh->hqk",
        one_hot,
        rel_bias,
        precision=lax.Precision.HIGHEST,
        preferred_element_type=jnp.float32,
    )


def norm_rows(values_in, gain):
    widened = values_in.astype(jnp.float32)
    scale = lax.rsqrt(jnp.mean(widened * widened, axis=-1, keepdims=True) + epsilon)
    return (widened * scale * gain).astype(jnp.bfloat16)


def layout(lengths_row, prefix_row, row_ids):
    req_ends = jnp.cumsum(lengths_row)
    req_starts = req_ends - lengths_row
    member = (
        (row_ids[:, None] >= req_starts[None, :]) & (row_ids[:, None] < req_ends[None, :])
    ).astype(jnp.int32)
    numbers = jnp.arange(lengths_row.shape[0], dtype=jnp.int32)
    req_index = jnp.sum(member * numbers[None, :], axis=1) + jnp.sum(member, axis=1) - 1
    offset = row_ids - jnp.sum(member * req_starts[None, :], axis=1)
    chosen = jnp.sum(member * prefix_row[None, :], axis=1)
    return (req_index, offset, chosen)


def softmax_part(scores, value_rows, allowed):
    scores = jnp.where(allowed[None], scores, masked_score)
    row_max = jnp.max(scores, axis=2)
    exp_terms = jnp.where(allowed[None], jnp.exp(scores - row_max[:, :, None]), 0.0)
    row_sum = jnp.sum(exp_terms, axis=2)
    weighted = jnp.einsum(
        "hqk,khd->hqd",
        exp_terms.astype(jnp.bfloat16),
        value_rows,
        preferred_element_type=jnp.float32,
    )
    return (row_max, row_sum, weighted)


def combine(first_part, second_part):
    row_max = jnp.maximum(first_part[0], second_part[0])
    scale_one = jnp.exp(first_part[0] - row_max)
    scale_two = jnp.exp(second_part[0] - row_max)
    row_sum = first_part[1] * scale_one + second_part[1] * scale_two
    weighted = first_part[2] * scale_one[:, :, None] + second_part[2] * scale_two[:, :, None]
    return (row_max, row_sum, weighted)


def feed_forward(rows_in, in_part, out_part):
    units = lax.dot_general(
        rows_in, in_part, (((1,), (1,)), ((), ())), preferred_element_type=jnp.float32
    )
    units = jnp.maximum(units, 0.0).astype(jnp.bfloat16)
    return jnp.dot(units, out_part, preferred_element_type=jnp.float32)


def body(
    tokens,
    attn_gain,
    w_query,
    w_key,
    w_value,
    w_attn_out,
    rel_bias,
    prefix_cache,
    lengths,
    prefix_map,
    mlp_gain,
    w_in,
    w_out,
):
    rows_here = tokens.shape[0]
    device_pos = lax.axis_index("req")
    group_lengths = lengths[0]
    group_map = prefix_map[0]
    normed = norm_rows(tokens, attn_gain)
    query = (
        jnp.dot(normed, w_query, preferred_element_type=jnp.float32)
        .astype(jnp.bfloat16)
        .reshape(rows_here, H, DK)
    )
    key_value = jnp.concatenate(
        [
            jnp.dot(normed, w_key, preferred_element_type=jnp.float32).astype(jnp.bfloat16),
            jnp.dot(normed, w_value, preferred_element_type=jnp.float32).astype(jnp.bfloat16),
        ],
        axis=1,
    )
    query_ids = device_pos * rows_here + jnp.arange(rows_here, dtype=jnp.int32)
    query_req, query_offset, query_prefix = layout(group_lengths, group_map, query_ids)
    all_positions = jnp.arange(PLEN, dtype=jnp.int32)
    prefix_bias = bias_lookup(all_positions[None, :] - PLEN - query_offset[:, None], rel_bias)
    empty_state = (
        jnp.full((H, rows_here), masked_score, jnp.float32),
        jnp.zeros((H, rows_here), jnp.float32),
        jnp.zeros((H, rows_here, DK), jnp.float32),
    )
    running = empty_state
    shard_kv = lax.all_gather(prefix_cache, "req", axis=1, tiled=True)
    prefix_ids = jnp.arange(PREF_GRP, dtype=jnp.int32)
    slices = shard_kv.shape[0]
    piece_len = shard_kv.shape[1]
    step_len = max(min(piece_len, 512 // slices), 1)
    for begin in range(0, piece_len, step_len):
        width = min(step_len, piece_len - begin)
        block = shard_kv[:, begin : begin + width]
        key_rows = block[:, :, :D].reshape(slices, width, H, DK)
        value_rows = block[:, :, D:].reshape(-1, H, DK)
        rel_terms = lax.dynamic_slice_in_dim(prefix_bias, begin, width, 2)
        prefix_scores = jnp.einsum(
            "qhd,swhd->hqsw", query, key_rows, preferred_element_type=jnp.float32
        )
        prefix_scores = (prefix_scores + rel_terms[:, :, None, :]).reshape(
            H, rows_here, slices * width
        )
        allowed = jnp.repeat(query_prefix[:, None] == prefix_ids[None, :], width, axis=1)
        running = combine(running, softmax_part(prefix_scores, value_rows, allowed))
    state = running
    window = padded(key_value, (("req", 0),), rows_here)
    window_ids = device_pos * rows_here - rows_here + jnp.arange(3 * rows_here, dtype=jnp.int32)
    window_req = layout(group_lengths, group_map, window_ids)[0]
    for part_idx in range(3):
        part_rows = window[part_idx * rows_here : (part_idx + 1) * rows_here]
        part_ids = window_ids[part_idx * rows_here : (part_idx + 1) * rows_here]
        part_req = window_req[part_idx * rows_here : (part_idx + 1) * rows_here]
        suffix_terms = bias_lookup(part_ids[None, :] - query_ids[:, None], rel_bias)
        suffix_allowed = part_req[None, :] == query_req[:, None]
        scores = (
            jnp.einsum(
                "qhd,khd->hqk",
                query,
                part_rows[:, :D].reshape(-1, H, DK),
                preferred_element_type=jnp.float32,
            )
            + suffix_terms
        )
        suffix_state = softmax_part(scores, part_rows[:, D:].reshape(-1, H, DK), suffix_allowed)
        state = combine(state, suffix_state)
    attended = (
        (state[2] / state[1][:, :, None])
        .transpose(1, 0, 2)
        .reshape(rows_here, D)
        .astype(jnp.bfloat16)
    )
    hidden_one = (
        tokens.astype(jnp.float32)
        + jnp.dot(attended, w_attn_out, preferred_element_type=jnp.float32)
    ).astype(jnp.bfloat16)
    normed_two = norm_rows(hidden_one, mlp_gain)
    gathered = lax.all_gather(normed_two, "grp", axis=0, tiled=True)
    mlp_total = lax.psum_scatter(
        feed_forward(gathered, w_in, w_out).astype(jnp.bfloat16),
        "grp",
        scatter_dimension=0,
        tiled=True,
    ).astype(jnp.float32)
    return (hidden_one.astype(jnp.float32) + mlp_total).astype(jnp.bfloat16)


def solution(mesh):
    return jax.shard_map(
        body,
        mesh=mesh,
        in_specs=(
            P(("grp", "req"), None),
            P(),
            P(),
            P(),
            P(),
            P(),
            P(),
            P("grp", "req", None),
            P("grp", None),
            P("grp", None),
            P(),
            P("grp", None),
            P("grp", None),
        ),
        out_specs=P(("grp", "req"), None),
        check_vma=False,
    )
```

profile of v0, /device:TPU:1, one launch (start us, length us, event | category | flops | bytes accessed | tf_op | source)
XLA Modules:
  0.0 308.1 jit_solution(4124527477737952821)
XLA Ops:
  14.9 5.5 %collective-permute-start = (bf16[128,2048]{1,0:T(8,128)(2,1)}, bf16[128,2048]{1,0:T(8,128)(2,1)}, u32[]{:S(2)}, u32[]{:S(2)}) collective-permute-start(bf16[128,2048]{1,0:T(8,128)(2,1)} %pad_maximum_fusion), channel_id=1, source_target_pairs={{0,1},{1,2},{2,3},{3,4},{4,5},{5,6},{6,7},{7,8},{8,9},{9,10},{10,1... | collective-permute-start | bytes 1572872 | tf_op jit(solution)/shard_map/ppermute | solution.py:23
  27.6 2.6 fusion.13
  31.5 3.0 fusion.10
  34.5 2.7 fusion.131
  41.0 2.6 copy.113
  43.6 4.1 %copy.94 = f32[16,128,256]{2,1,0:T(8,128)} copy(f32[16,128,256]{2,0,1:T(8,128)} %get-tuple-element.28) | data formatting | bytes 4194304 | tf_op jit(solution)/shard_map/dynamic_slice | solution.py:151
  47.7 2.5 copy.105
  50.3 4.2 %copy.100 = f32[16,128,256]{2,1,0:T(8,128)} copy(f32[16,128,256]{2,0,1:T(8,128)} %get-tuple-element.29) | data formatting | bytes 4194304 | tf_op jit(solution)/shard_map/dynamic_slice | solution.py:151
  70.1 97.0 %all-gather.3.cloned.1.call-done = bf16[2,512,2048]{2,0,1:T(2,128)(2,1)} async-done(((bf16[2,16,2048]{2,0,1:T(2,128)(2,1)}), bf16[2,512,2048]{2,0,1:T(2,128)(2,1)}) %all-gather.3.cloned.1.call-update) | async-done | bytes 4194320 | tf_op jit(solution)/shard_map/all_gather | solution.py:141
  167.1 5.7 %fusion.130 = (bf16[2,256,1024]{2,0,1:T(2,128)(2,1)}, bf16[2,256,1024]{2,0,1:T(2,128)(2,1)}, bf16[2,256,1024]{2,0,1:T(2,128)(2,1)}, bf16[2,256,1024]{2,0,1:T(2,128)(2,1)}) fusion(bf16[2,512,2048]{2,0,1:T(2,128)(2,1)} %all-gather.3.cloned.1.call-done), kind=kLoop, calls=%fused_computation.203 | loop fusion | bytes 8388608 | tf_op jit(solution)/shard_map/slice | solution.py:150
  172.8 3.6 %copy.122 = bf16[2,256,1024]{1,2,0:T(8,128)(2,1)} copy(bf16[2,256,1024]{2,0,1:T(2,128)(2,1)} %get-tuple-element.25) | data formatting | bytes 2097152
  176.4 3.7 %copy.123 = bf16[2,256,1024]{1,2,0:T(8,128)(2,1)} copy(bf16[2,256,1024]{2,0,1:T(2,128)(2,1)} %get-tuple-element.27) | data formatting | bytes 2097152
  180.1 2.9 select_reduce_fusion.3
  183.0 2.4 select_reduce_fusion.1
  188.7 5.3 %copy.101 = f32[16,128,2,256]{1,3,2,0:T(8,128)} copy(f32[16,128,2,256]{3,1,2,0:T(8,128)} %copy-done.2) | data formatting | bytes 8388608 | tf_op jit(solution)/shard_map/add | solution.py:155
  194.0 5.3 %copy.95 = f32[16,128,2,256]{1,3,2,0:T(8,128)} copy(f32[16,128,2,256]{3,1,2,0:T(8,128)} %copy-done.1) | data formatting | bytes 8388608 | tf_op jit(solution)/shard_map/add | solution.py:155
  199.3 4.9 %copy.96 = bf16[2,256,1024]{1,0,2:T(2,128)(2,1)} copy(bf16[2,256,1024]{2,0,1:T(2,128)(2,1)} %get-tuple-element.26) | data formatting | bytes 2097152 | tf_op jit(solution)/shard_map/slice | solution.py:150
  204.2 2.6 reshape.536
  206.8 4.9 %copy.102 = bf16[2,256,1024]{1,0,2:T(2,128)(2,1)} copy(bf16[2,256,1024]{2,0,1:T(2,128)(2,1)} %get-tuple-element.24) | data formatting | bytes 2097152 | tf_op jit(solution)/shard_map/slice | solution.py:150
  211.6 2.6 reshape.539
  216.9 5.3 %fusion.4 = (bf16[16,128,512]{1,2,0:T(8,128)(2,1)S(1)}, bf16[16,128,512]{1,2,0:T(8,128)(2,1)S(1)}) fusion(f32[16,128,2,256]{1,3,2,0:T(8,128)} %copy.101, f32[16,128]{1,0:T(8,128)S(1)} %get-tuple-element.12, pred[128,512]{0,1:T(8,128)(4,1)S(1)} %bitcast.222, f32[16,128]{1,0:T(8,128)S(1)} %get-tuple-element.61, f32[16,128,2,256]{1,3,2,0:T(8,128)} %copy.95), kind=kLoop, calls=%fused_computation.6 | loop fusion | flops 8388608 | bytes 12664832 | tf_op jit(solution)/shard_map/convert_element_type | solution.py:75
  227.2 36.3 %all-gather.5.cloned.1.call-done = bf16[512,1024]{1,0:T(8,128)(2,1)} async-done(((bf16[128,1024]{1,0:T(8,128)(2,1)}), bf16[512,1024]{1,0:T(8,128)(2,1)}) %all-gather.5.cloned.1.call-update) | async-done | bytes 1048592 | tf_op jit(solution)/shard_map/all_gather | solution.py:192
  263.6 5.3 %convolution_convert_fusion = bf16[512,1024]{1,0:T(8,128)(2,1)} fusion(bf16[1024,1024]{1,0:T(8,128)(2,1)S(1)} %copy-done, bf16[512,1024]{1,0:T(8,128)(2,1)} %all-gather.5.cloned.1.call-done, bf16[1024,1024]{1,0:T(8,128)(2,1)} %param.24), kind=kOutput, calls=%fused_computation.27 | convolution fusion | flops 2149056512 | bytes 6291456 | tf_op jit(solution)/shard_map/dot_general | solution.py:96
  268.9 31.0 %reduce-scatter.2.cloned.1.call-done = bf16[128,1024]{1,0:T(8,128)(2,1)} async-done(((bf16[512,1024]{1,0:T(8,128)(2,1)}), bf16[128,1024]{1,0:T(8,128)(2,1)}) %reduce-scatter.2.cloned.1.call-update) | async-done | bytes 262160 | tf_op jit(solution)/shard_map/reduce_scatter | solution.py:193
  (118 shorter events, 48.6 us)
Async XLA Ops:
  6.5 257.0 %copy-start = (bf16[1024,1024]{1,0:T(8,128)(2,1)S(1)}, bf16[1024,1024]{1,0:T(8,128)(2,1)}, u32[]{:S(2)}) copy-start(bf16[1024,1024]{1,0:T(8,128)(2,1)} %param.25) | copy-start | bytes 6291460
  6.5 5.4 %copy-start.4 = (bf16[128,1024]{1,0:T(8,128)(2,1)S(1)}, bf16[128,1024]{1,0:T(8,128)(2,1)}, u32[]{:S(2)}) copy-start(bf16[128,1024]{1,0:T(8,128)(2,1)} %param.13) | copy-start | bytes 786436
  6.5 5.4 %copy-start.21 = (f32[1024]{0:T(1024)S(1)}, f32[1024]{0:T(1024)}, u32[]{:S(2)}) copy-start(f32[1024]{0:T(1024)} %param.14) | copy-start | bytes 12292
  6.5 160.6 %all-gather.3.cloned.1.call-start = ((), (), s32[]{:S(2)}) async-start(), calls=%async_computation.1 | async-start | bytes 4325376 | tf_op jit(solution)/shard_map/all_gather | solution.py:141
  8.4 255.2 %all-gather.5.cloned.1.call-start = ((), (), s32[]{:S(2)}) async-start(), calls=%async_computation.2 | async-start | bytes 1310720 | tf_op jit(solution)/shard_map/all_gather | solution.py:192
  8.5 3.5 %copy-start.13 = (bf16[1024,1024]{1,0:T(8,128)(2,1)S(1)}, bf16[1024,1024]{1,0:T(8,128)(2,1)}, u32[]{:S(2)}) copy-start(bf16[1024,1024]{1,0:T(8,128)(2,1)} %param.16) | copy-start | bytes 6291460
  13.5 10.0 %copy-start.25 = (s32[1,64]{1,0:T(1,128)S(1)}, s32[1,64]{1,0:T(1,128)}, u32[]{:S(2)}) copy-start(s32[1,64]{1,0:T(1,128)} %param.21) | copy-start | bytes 772
  13.5 11.2 %copy-start.20 = (f32[32,16]{0,1:T(8,128)S(1)}, f32[32,16]{0,1:T(8,128)}, u32[]{:S(2)}) copy-start(f32[32,16]{0,1:T(8,128)} %param.19) | copy-start | bytes 6148
  13.5 40.9 %collective-permute-start.1 = (bf16[128,2048]{1,0:T(8,128)(2,1)}, bf16[128,2048]{1,0:T(8,128)(2,1)}, u32[]{:S(2)}, u32[]{:S(2)}) collective-permute-start(bf16[128,2048]{1,0:T(8,128)(2,1)} %pad_maximum_fusion), channel_id=1, source_target_pairs={{1,0},{2,1},{3,2},{4,3},{5,4},{6,5},{7,6},{8,7},{9,8},{10,9},{11,1... | collective-permute-start | bytes 1572872 | tf_op jit(solution)/shard_map/ppermute | solution.py:24
  14.9 45.0 %collective-permute-start = (bf16[128,2048]{1,0:T(8,128)(2,1)}, bf16[128,2048]{1,0:T(8,128)(2,1)}, u32[]{:S(2)}, u32[]{:S(2)}) collective-permute-start(bf16[128,2048]{1,0:T(8,128)(2,1)} %pad_maximum_fusion), channel_id=1, source_target_pairs={{0,1},{1,2},{2,3},{3,4},{4,5},{5,6},{6,7},{7,8},{8,9},{9,10},{10,1... | collective-permute-start | bytes 1572872 | tf_op jit(solution)/shard_map/ppermute | solution.py:23
  23.3 3.6 %copy-start.26 = (s32[1,64]{1,0:T(1,128)S(1)}, s32[1,64]{1,0:T(1,128)}, u32[]{:S(2)}) copy-start(s32[1,64]{1,0:T(1,128)} %param.22) | copy-start | bytes 772
  26.9 3.3 %copy-start.9 = (f32[128,128,16]{0,1,2:T(8,128)S(1)}, f32[128,128,16]{0,1,2:T(8,128)}, u32[]{:S(2)}) copy-start(f32[128,128,16]{0,1,2:T(8,128)} %copy.109) | copy-start | bytes 3145732
  54.4 131.1 %copy-start.22 = (pred[128,2]{0,1:T(4,128)(4,1)}, pred[128,2]{0,1:T(4,128)(4,1)S(1)}, u32[]{:S(2)}) copy-start(pred[128,2]{0,1:T(4,128)(4,1)S(1)} %iota_compare_fusion.10) | copy-start | bytes 772
  65.3 3.2 %copy-start.10 = (f32[128,128,16]{0,1,2:T(8,128)S(1)}, f32[128,128,16]{0,1,2:T(8,128)}, u32[]{:S(2)}) copy-start(f32[128,128,16]{0,1,2:T(8,128)} %copy.105) | copy-start | bytes 3145732
  65.3 3.2 %copy-start.17 = (bf16[128,1024]{0,1:T(8,128)(2,1)S(1)}, bf16[128,1024]{0,1:T(8,128)(2,1)}, u32[]{:S(2)}) copy-start(bf16[128,1024]{0,1:T(8,128)(2,1)} %copy.104) | copy-start | bytes 786436
  180.1 2.9 copy-start.15
  180.1 2.9 copy-start.18
  183.0 2.5 copy-start.1
  185.5 2.0 copy-start.2
  211.6 4.9 %copy-start.16 = (bf16[128,1024]{0,1:T(8,128)(2,1)S(1)}, bf16[128,1024]{0,1:T(8,128)(2,1)}, u32[]{:S(2)}) copy-start(bf16[128,1024]{0,1:T(8,128)(2,1)} %copy.110) | copy-start | bytes 786436
  214.2 2.6 copy-start.23
  216.8 5.4 %copy-start.6 = (bf16[512,16,64]{0,2,1:T(8,128)(2,1)S(1)}, bf16[512,16,64]{0,2,1:T(8,128)(2,1)}, u32[]{:S(2)}) copy-start(bf16[512,16,64]{0,2,1:T(8,128)(2,1)} %reshape.536) | copy-start | bytes 3145732
  224.0 1.8 copy-start.14
  227.2 72.7 %reduce-scatter.2.cloned.1.call-start = ((), (), s32[]{:S(2)}) async-start(), calls=%async_computation.3 | async-start | bytes 1310720 | tf_op jit(solution)/shard_map/reduce_scatter | solution.py:193
  (8 other events, 8.8 us)
Sparse Core Ops, SparseCore 0:
  9.0 158.0 all-gather.2
  227.3 36.2 all-gather.4
  269.0 30.7 reduce-scatter.1
where the time goes:
time: 309 us; the launch traced here: 308 us
  waiting for transfers between devices  164 us (53%)
  local copies, waits for them, and re-layouts  78 us (25%)
  matrix products  30.9 us (10%)
  other arithmetic  14.2 us (5%)
  between operations  13.5 us (4%)
  starting transfers between devices  6.96 us (2%)
    all_gather x1, waiting for transfers between devices, body(): shard_kv = lax.all_gather(prefix_cache, 'req', axis=1, tiled=True)  97 us
    all_gather x1, waiting for transfers between devices, body(): gathered = lax.all_gather(normed_two, 'grp', axis=0, tiled=True)  36.3 us
    reduce_scatter x1, waiting for transfers between devices, body(): lax.psum_scatter(feed_forward(gathered, w_in, w_out).astype(jnp.bfloat16)...  31 us
    unnamed x57, local copies, waits for them, and re-layouts  15.5 us
    slice x3, local copies, waits for them, and re-layouts, body(): value_rows = block[:, :, D:].reshape(-1, H, DK)  15.4 us
    dynamic_slice x3, local copies, waits for them, and re-layouts, body(): rel_terms = lax.dynamic_slice_in_dim(prefix_bias, begin, width, 2)  11 us
    add x2, local copies, waits for them, and re-layouts, body(): prefix_scores + rel_terms[:, :, None, :]  10.6 us
    dot_general x4, matrix products, bias_lookup(): jnp.einsum('qkb,bh->hqk', one_hot, rel_bias, precision=lax.Precision.HIGH...  8.1 us
  transfers between devices with their start and end apart: 5, of which 3 were waited for; matrix products, arithmetic and copies ran while one was open for 17% of the time, Pallas kernels for 0%

commit v1 on v0

--- a/solution.py
+++ b/solution.py
@@ -138,7 +138,9 @@
         jnp.zeros((H, rows_here, DK), jnp.float32),
     )
     running = empty_state
-    shard_kv = lax.all_gather(prefix_cache, "req", axis=1, tiled=True)
+    shard_kv = jnp.concatenate(
+        lax.all_to_all(jnp.stack([prefix_cache] * lax.axis_size("req")), "req", 0, 0), axis=1
+    )
     prefix_ids = jnp.arange(PREF_GRP, dtype=jnp.int32)
     slices = shard_kv.shape[0]
     piece_len = shard_kv.shape[1]

time: 309 us -> 212 us (0.69)
  waiting for transfers between devices: 164 us -> 61.2 us
  starting transfers between devices: 6.96 us -> 18.2 us
  local copies, waits for them, and re-layouts: 78 us -> 72.5 us
    all_gather x1 -> x0, waiting for transfers between devices: 97 us -> none  [body(): shard_kv = lax.all_gather(prefix_cache, 'req', axis=1, tiled=True)]
    all_to_all x0 -> x1, starting transfers between devices: none -> 11.4 us  [body(): lax.all_to_all(jnp.stack([prefix_cache] * lax.axis_size('req')), 'req', 0...]
    all_gather x1, waiting for transfers between devices: 36.3 us -> 25 us  [body(): gathered = lax.all_gather(normed_two, 'grp', axis=0, tiled=True)]
    unnamed x57 -> x56, local copies, waits for them, and re-layouts: 15.5 us -> 6.3 us
    slice x3, local copies, waits for them, and re-layouts: 15.4 us -> 9.44 us  [body(): value_rows = block[:, :, D:].reshape(-1, H, DK)]
    all_to_all x0 -> x1, waiting for transfers between devices: none -> 5.23 us  [body(): lax.all_to_all(jnp.stack([prefix_cache] * lax.axis_size('req')), 'req', 0...]
    slice x0 -> x2, local copies, waits for them, and re-layouts: none -> 4.56 us  [body(): key_rows = block[:, :, :D].reshape(slices, width, H, DK)]
  transfers between devices with their start and end apart: 5 -> 5, of which waited for: 3 -> 3; matrix products, arithmetic and copies ran while one was open for 17% -> 24% of each run, Pallas kernels for 0% -> 0%
where the time goes in v1:
time: 212 us; the launch traced here: 211 us
  local copies, waits for them, and re-layouts  72.5 us (34%)
  waiting for transfers between devices  61.2 us (29%)
  matrix products  31 us (15%)
  starting transfers between devices  18.2 us (9%)
  other arithmetic  14.3 us (7%)
  between operations  13.9 us (7%)
    reduce_scatter x1, waiting for transfers between devices, body(): lax.psum_scatter(feed_forward(gathered, w_in, w_out).astype(jnp.bfloat16)...  31 us
    all_gather x1, waiting for transfers between devices, body(): gathered = lax.all_gather(normed_two, 'grp', axis=0, tiled=True)  25 us
    all_to_all x1, starting transfers between devices, body(): lax.all_to_all(jnp.stack([prefix_cache] * lax.axis_size('req')), 'req', 0...  11.4 us
    dynamic_slice x3, local copies, waits for them, and re-layouts, body(): rel_terms = lax.dynamic_slice_in_dim(prefix_bias, begin, width, 2)  11.1 us
    add x2, local copies, waits for them, and re-layouts, body(): prefix_scores + rel_terms[:, :, None, :]  10.6 us
    slice x3, local copies, waits for them, and re-layouts, body(): value_rows = block[:, :, D:].reshape(-1, H, DK)  9.44 us
    dot_general x4, matrix products, bias_lookup(): jnp.einsum('qkb,bh->hqk', one_hot, rel_bias, precision=lax.Precision.HIGH...  8.14 us
    dot_general x3, local copies, waits for them, and re-layouts, bias_lookup(): jnp.einsum('qkb,bh->hqk', one_hot, rel_bias, precision=lax.Precision.HIGH...  6.53 us
  transfers between devices with their start and end apart: 5, of which 3 were waited for; matrix products, arithmetic and copies ran while one was open for 24% of the time, Pallas kernels for 0%

profile of v1, /device:TPU:1, one launch (start us, length us, event | category | flops | bytes accessed | tf_op | source)
XLA Modules:
  0.0 211.1 jit_solution(5509230421827168940)
XLA Ops:
  12.9 5.5 %collective-permute-start = (bf16[128,2048]{1,0:T(8,128)(2,1)}, bf16[128,2048]{1,0:T(8,128)(2,1)}, u32[]{:S(2)}, u32[]{:S(2)}) collective-permute-start(bf16[128,2048]{1,0:T(8,128)(2,1)} %pad_maximum_fusion), channel_id=1, source_target_pairs={{0,1},{1,2},{2,3},{3,4},{4,5},{5,6},{6,7},{7,8},{8,9},{9,10},{10,1... | collective-permute-start | bytes 1572872 | tf_op jit(solution)/shard_map/ppermute | solution.py:23
  18.4 2.5 %stack.2 = bf16[32,2,16,2048]{3,2,1,0:T(8,128)(2,1)} broadcast(bf16[2,16,2048]{2,1,0:T(8,128)(2,1)S(1)} %copy-done.21), dimensions={1,2,3} | broadcast | bytes 4325376 | tf_op jit(solution)/shard_map/stack | solution.py:142
  20.9 11.4 %all-to-all-start = ((bf16[32,2,16,2048]{3,2,1,0:T(8,128)(2,1)}), bf16[32,2,16,2048]{3,2,1,0:T(8,128)(2,1)}, u32[]{:S(2)}, u32[]{:S(2)}) async-start(bf16[32,2,16,2048]{3,2,1,0:T(8,128)(2,1)} %stack.2), calls=%async_computation | async-start | bytes 8388608 | tf_op jit(solution)/shard_map/all_to_all | solution.py:142
  39.6 2.7 %fusion.13 = f32[128,128,16]{1,2,0:T(8,128)} fusion(s32[128,128]{1,0:T(8,128)} %get-tuple-element.57, f32[32,16]{0,1:T(8,128)S(1)} %copy-done.20), kind=kOutput, calls=%fused_computation.26 | convolution fusion | flops 101187584 | bytes 1116160 | tf_op jit(solution)/shard_map/qkb,bh->hqk/dot_general | solution.py:40
  43.6 3.0 %fusion.10 = f32[16,128,512]{2,0,1:T(8,128)S(1)} fusion(s32[128,512]{1,0:T(8,128)S(1)} %fusion.68, f32[32,16]{0,1:T(8,128)S(1)} %copy-done.20), kind=kOutput, calls=%fused_computation.17 | convolution fusion | flops 404750336 | bytes 4458496 | tf_op jit(solution)/shard_map/qkb,bh->hqk/dot_general | solution.py:40
  46.6 2.7 %fusion.131 = (f32[16,128,256]{2,0,1:T(8,128)}, f32[16,128,256]{2,0,1:T(8,128)}) fusion(f32[16,128,512]{2,0,1:T(8,128)S(1)} %fusion.10), kind=kLoop, calls=%fused_computation.204 | loop fusion | bytes 8388608 | tf_op jit(solution)/shard_map/dynamic_slice | solution.py:153
  53.0 2.6 %copy.113 = f32[128,128,16]{0,1,2:T(8,128)} copy(f32[128,128,16]{1,2,0:T(8,128)} %fusion.13) | data formatting | bytes 2097152 | tf_op jit(solution)/shard_map/qkb,bh->hqk/dot_general | solution.py:40
  55.6 4.2 %copy.94 = f32[16,128,256]{2,1,0:T(8,128)} copy(f32[16,128,256]{2,0,1:T(8,128)} %get-tuple-element.28) | data formatting | bytes 4194304 | tf_op jit(solution)/shard_map/dynamic_slice | solution.py:153
  59.8 2.6 %copy.105 = f32[128,128,16]{0,1,2:T(8,128)} copy(f32[128,128,16]{1,2,0:T(8,128)} %fusion.11) | data formatting | bytes 2097152 | tf_op jit(solution)/shard_map/qkb,bh->hqk/dot_general | solution.py:40
  62.3 4.2 %copy.100 = f32[16,128,256]{2,1,0:T(8,128)} copy(f32[16,128,256]{2,0,1:T(8,128)} %get-tuple-element.29) | data formatting | bytes 4194304 | tf_op jit(solution)/shard_map/dynamic_slice | solution.py:153
  82.2 5.2 %all-to-all-done = bf16[32,2,16,2048]{3,2,1,0:T(8,128)(2,1)} async-done(((bf16[32,2,16,2048]{3,2,1,0:T(8,128)(2,1)}), bf16[32,2,16,2048]{3,2,1,0:T(8,128)(2,1)}, u32[]{:S(2)}, u32[]{:S(2)}) %all-to-all-start) | async-done | bytes 4194336 | tf_op jit(solution)/shard_map/all_to_all | solution.py:142
  87.4 2.5 %copy.91 = bf16[32,2,16,2048]{3,2,0,1:T(8,128)(2,1)S(1)} copy(bf16[32,2,16,2048]{3,2,1,0:T(8,128)(2,1)} %all-to-all-done) | data formatting | bytes 8388608 | tf_op jit(solution)/shard_map/all_to_all | solution.py:142
  96.6 2.9 %select_reduce_fusion.3 = (f32[16,128]{1,0:T(8,128)S(1)}, f32[16,128,2,256]{3,1,2,0:T(8,128)S(1)}) fusion(pred[128,2]{0,1:T(4,128)(4,1)S(1)} %iota_compare_fusion.10, f32[16,128,256]{2,1,0:T(8,128)} %copy.94, bf16[128,16,64,1]{0,2,3,1:T(8,128)(2,1)S(1)} %bitcast.217, bf16[2,256,16,64]{1,3,2,0:T(8,128)(2,1)} %bitcast.219), kind=kOutput, calls=%fused_computation.16 | convolution fusion | flops 137361408 | bytes 7610624 | tf_op jit(solution)/shard_map/qhd,swhd->hqsw/dot_general | solution.py:154
  99.5 2.4 %select_reduce_fusion.1 = (f32[16,128]{1,0:T(8,128)}, f32[16,128]{1,0:T(8,128)S(1)}, f32[16,128,2,256]{3,1,2,0:T(8,128)S(1)}) fusion(f32[16,128,2,256]{3,1,2,0:T(8,128)S(1)} %get-tuple-element.62, f32[16,128]{1,0:T(8,128)S(1)} %get-tuple-element.61, pred[128,2]{0,1:T(4,128)(4,1)S(1)} %iota_compare_fusion.10, f32[16,128,256]{2,1,0:T(8,128)S(1)} %copy-done.15, ...), kind=kOutput, calls=%fused_computation.13 | convolution fusion | flops 141553664 | bytes 11821312 | tf_op jit(solution)/shard_map/qhd,swhd->hqsw/dot_general | solution.py:154
  105.2 5.3 %copy.101 = f32[16,128,2,256]{1,3,2,0:T(8,128)} copy(f32[16,128,2,256]{3,1,2,0:T(8,128)} %copy-done.2) | data formatting | bytes 8388608 | tf_op jit(solution)/shard_map/add | solution.py:157
  110.5 5.3 %copy.95 = f32[16,128,2,256]{1,3,2,0:T(8,128)} copy(f32[16,128,2,256]{3,1,2,0:T(8,128)} %copy-done.1) | data formatting | bytes 8388608 | tf_op jit(solution)/shard_map/add | solution.py:157
  115.8 3.7 %copy.96 = bf16[2,256,1024]{1,0,2:T(2,128)(2,1)} copy(bf16[2,256,1024]{2,1,0:T(8,128)(2,1)} %get-tuple-element.26) | data formatting | bytes 2097152 | tf_op jit(solution)/shard_map/slice | solution.py:152
  119.5 2.6 %reshape.546 = bf16[512,16,64]{0,2,1:T(8,128)(2,1)} reshape(bf16[2,256,1024]{1,0,2:T(2,128)(2,1)} %copy.96) | data formatting | bytes 2097152 | tf_op jit(solution)/shard_map/reshape | solution.py:152
  122.1 3.7 %copy.102 = bf16[2,256,1024]{1,0,2:T(2,128)(2,1)} copy(bf16[2,256,1024]{2,1,0:T(8,128)(2,1)} %get-tuple-element.24) | data formatting | bytes 2097152 | tf_op jit(solution)/shard_map/slice | solution.py:152
  125.7 2.6 %reshape.549 = bf16[512,16,64]{0,2,1:T(8,128)(2,1)} reshape(bf16[2,256,1024]{1,0,2:T(2,128)(2,1)} %copy.102) | data formatting | bytes 2097152 | tf_op jit(solution)/shard_map/reshape | solution.py:152
  130.9 5.3 %fusion.4 = (bf16[16,128,512]{1,2,0:T(8,128)(2,1)S(1)}, bf16[16,128,512]{1,2,0:T(8,128)(2,1)S(1)}) fusion(f32[16,128,2,256]{1,3,2,0:T(8,128)} %copy.101, f32[16,128]{1,0:T(8,128)S(1)} %get-tuple-element.12, pred[128,512]{0,1:T(8,128)(4,1)S(1)} %bitcast.226, f32[16,128]{1,0:T(8,128)S(1)} %get-tuple-element.61, f32[16,128,2,256]{1,3,2,0:T(8,128)} %copy.95), kind=kLoop, calls=%fused_computation.6 | loop fusion | flops 8388608 | bytes 12664832 | tf_op jit(solution)/shard_map/convert_element_type | solution.py:75
  141.3 25.0 %all-gather.2.cloned.1.call-done = bf16[512,1024]{1,0:T(8,128)(2,1)} async-done(((bf16[128,1024]{1,0:T(8,128)(2,1)}), bf16[512,1024]{1,0:T(8,128)(2,1)}) %all-gather.2.cloned.1.call-update) | async-done | bytes 1048592 | tf_op jit(solution)/shard_map/all_gather | solution.py:194
  166.3 5.3 %convolution_convert_fusion = bf16[512,1024]{1,0:T(8,128)(2,1)} fusion(bf16[1024,1024]{1,0:T(8,128)(2,1)S(1)} %copy-done, bf16[512,1024]{1,0:T(8,128)(2,1)} %all-gather.2.cloned.1.call-done, bf16[1024,1024]{1,0:T(8,128)(2,1)} %param.24), kind=kOutput, calls=%fused_computation.27 | convolution fusion | flops 2149056512 | bytes 6291456 | tf_op jit(solution)/shard_map/dot_general | solution.py:96
  171.6 31.0 %reduce-scatter.2.cloned.1.call-done = bf16[128,1024]{1,0:T(8,128)(2,1)} async-done(((bf16[512,1024]{1,0:T(8,128)(2,1)}), bf16[128,1024]{1,0:T(8,128)(2,1)}) %reduce-scatter.2.cloned.1.call-update) | async-done | bytes 262160 | tf_op jit(solution)/shard_map/reduce_scatter | solution.py:195
  (120 shorter events, 53.3 us)
Async XLA Ops:
  6.5 159.8 %copy-start = (bf16[1024,1024]{1,0:T(8,128)(2,1)S(1)}, bf16[1024,1024]{1,0:T(8,128)(2,1)}, u32[]{:S(2)}) copy-start(bf16[1024,1024]{1,0:T(8,128)(2,1)} %param.25) | copy-start | bytes 6291460
  6.5 3.5 %copy-start.4 = (bf16[128,1024]{1,0:T(8,128)(2,1)S(1)}, bf16[128,1024]{1,0:T(8,128)(2,1)}, u32[]{:S(2)}) copy-start(bf16[128,1024]{1,0:T(8,128)(2,1)} %param.13) | copy-start | bytes 786436
  6.5 3.5 %copy-start.22 = (f32[1024]{0:T(1024)S(1)}, f32[1024]{0:T(1024)}, u32[]{:S(2)}) copy-start(f32[1024]{0:T(1024)} %param.14) | copy-start | bytes 12292
  6.5 3.5 %copy-start.13 = (bf16[1024,1024]{1,0:T(8,128)(2,1)S(1)}, bf16[1024,1024]{1,0:T(8,128)(2,1)}, u32[]{:S(2)}) copy-start(bf16[1024,1024]{1,0:T(8,128)(2,1)} %param.16) | copy-start | bytes 6291460
  10.1 8.3 %copy-start.21 = (bf16[2,16,2048]{2,1,0:T(8,128)(2,1)S(1)}, bf16[2,16,2048]{2,1,0:T(8,128)(2,1)}, u32[]{:S(2)}) copy-start(bf16[2,16,2048]{2,1,0:T(8,128)(2,1)} %param.20) | copy-start | bytes 393220
  11.6 54.9 %collective-permute-start.1 = (bf16[128,2048]{1,0:T(8,128)(2,1)}, bf16[128,2048]{1,0:T(8,128)(2,1)}, u32[]{:S(2)}, u32[]{:S(2)}) collective-permute-start(bf16[128,2048]{1,0:T(8,128)(2,1)} %pad_maximum_fusion), channel_id=1, source_target_pairs={{1,0},{2,1},{3,2},{4,3},{5,4},{6,5},{7,6},{8,7},{9,8},{10,9},{11,1... | collective-permute-start | bytes 1572872 | tf_op jit(solution)/shard_map/ppermute | solution.py:24
  12.9 59.0 %collective-permute-start = (bf16[128,2048]{1,0:T(8,128)(2,1)}, bf16[128,2048]{1,0:T(8,128)(2,1)}, u32[]{:S(2)}, u32[]{:S(2)}) collective-permute-start(bf16[128,2048]{1,0:T(8,128)(2,1)} %pad_maximum_fusion), channel_id=1, source_target_pairs={{0,1},{1,2},{2,3},{3,4},{4,5},{5,6},{6,7},{7,8},{8,9},{9,10},{10,1... | collective-permute-start | bytes 1572872 | tf_op jit(solution)/shard_map/ppermute | solution.py:23
  20.9 66.5 %all-to-all-start = ((bf16[32,2,16,2048]{3,2,1,0:T(8,128)(2,1)}), bf16[32,2,16,2048]{3,2,1,0:T(8,128)(2,1)}, u32[]{:S(2)}, u32[]{:S(2)}) async-start(bf16[32,2,16,2048]{3,2,1,0:T(8,128)(2,1)} %stack.2), calls=%async_computation | async-start | bytes 8388608 | tf_op jit(solution)/shard_map/all_to_all | solution.py:142
  32.3 3.2 %copy-start.26 = (s32[1,64]{1,0:T(1,128)S(1)}, s32[1,64]{1,0:T(1,128)}, u32[]{:S(2)}) copy-start(s32[1,64]{1,0:T(1,128)} %param.21) | copy-start | bytes 772
  32.3 3.6 %copy-start.27 = (s32[1,64]{1,0:T(1,128)S(1)}, s32[1,64]{1,0:T(1,128)}, u32[]{:S(2)}) copy-start(s32[1,64]{1,0:T(1,128)} %param.22) | copy-start | bytes 772
  32.3 4.6 %copy-start.20 = (f32[32,16]{0,1:T(8,128)S(1)}, f32[32,16]{0,1:T(8,128)}, u32[]{:S(2)}) copy-start(f32[32,16]{0,1:T(8,128)} %param.19) | copy-start | bytes 6148
  32.3 134.0 %all-gather.2.cloned.1.call-start = ((), (), s32[]{:S(2)}) async-start(), calls=%async_computation.2 | async-start | bytes 1310720 | tf_op jit(solution)/shard_map/all_gather | solution.py:194
  39.1 3.2 %copy-start.10 = (f32[128,128,16]{0,1,2:T(8,128)S(1)}, f32[128,128,16]{0,1,2:T(8,128)}, u32[]{:S(2)}) copy-start(f32[128,128,16]{0,1,2:T(8,128)} %copy.109) | copy-start | bytes 3145732
  66.5 35.5 %copy-start.23 = (pred[128,2]{0,1:T(4,128)(4,1)}, pred[128,2]{0,1:T(4,128)(4,1)S(1)}, u32[]{:S(2)}) copy-start(pred[128,2]{0,1:T(4,128)(4,1)S(1)} %iota_compare_fusion.10) | copy-start | bytes 772
  77.4 3.2 %copy-start.9 = (f32[128,128,16]{0,1,2:T(8,128)S(1)}, f32[128,128,16]{0,1,2:T(8,128)}, u32[]{:S(2)}) copy-start(f32[128,128,16]{0,1,2:T(8,128)} %copy.105) | copy-start | bytes 3145732
  77.4 3.2 %copy-start.17 = (bf16[128,1024]{0,1:T(8,128)(2,1)S(1)}, bf16[128,1024]{0,1:T(8,128)(2,1)}, u32[]{:S(2)}) copy-start(bf16[128,1024]{0,1:T(8,128)(2,1)} %copy.104) | copy-start | bytes 786436
  96.6 2.9 %copy-start.15 = (f32[16,128,256]{2,1,0:T(8,128)S(1)}, f32[16,128,256]{2,1,0:T(8,128)}, u32[]{:S(2)}) copy-start(f32[16,128,256]{2,1,0:T(8,128)} %copy.100) | copy-start | bytes 6291460
  96.6 2.9 %copy-start.18 = (bf16[2,256,1024]{1,2,0:T(8,128)(2,1)S(1)}, bf16[2,256,1024]{1,2,0:T(8,128)(2,1)}, u32[]{:S(2)}) copy-start(bf16[2,256,1024]{1,2,0:T(8,128)(2,1)} %copy.98) | copy-start | bytes 3145732
  99.5 2.5 %copy-start.1 = (f32[16,128,2,256]{3,1,2,0:T(8,128)}, f32[16,128,2,256]{3,1,2,0:T(8,128)S(1)}, u32[]{:S(2)}) copy-start(f32[16,128,2,256]{3,1,2,0:T(8,128)S(1)} %get-tuple-element.62) | copy-start | bytes 12582916
  102.0 2.0 copy-start.2
  125.7 4.9 %copy-start.16 = (bf16[128,1024]{0,1:T(8,128)(2,1)S(1)}, bf16[128,1024]{0,1:T(8,128)(2,1)}, u32[]{:S(2)}) copy-start(bf16[128,1024]{0,1:T(8,128)(2,1)} %copy.110) | copy-start | bytes 786436
  128.3 2.6 %copy-start.24 = (pred[128,2]{0,1:T(4,128)(4,1)S(1)}, pred[128,2]{0,1:T(4,128)(4,1)}, u32[]{:S(2)}) copy-start(pred[128,2]{0,1:T(4,128)(4,1)} %copy-done.23) | copy-start | bytes 772
  130.9 5.4 %copy-start.6 = (bf16[512,16,64]{0,2,1:T(8,128)(2,1)S(1)}, bf16[512,16,64]{0,2,1:T(8,128)(2,1)}, u32[]{:S(2)}) copy-start(bf16[512,16,64]{0,2,1:T(8,128)(2,1)} %reshape.546) | copy-start | bytes 3145732
  141.2 61.3 %reduce-scatter.2.cloned.1.call-start = ((), (), s32[]{:S(2)}) async-start(), calls=%async_computation.3 | async-start | bytes 1310720 | tf_op jit(solution)/shard_map/reduce_scatter | solution.py:195
  (9 other events, 10.5 us)
Sparse Core Ops, SparseCore 0:
  141.4 24.8 all-gather.1
  171.7 30.7 reduce-scatter.1
